TPU v7x, 512 devices: a whole 4x8x8 slice. The times are simulated.
512 devices in a mesh: row: 16 (over z, core), col: 32 (over x, y).
Axes of the slice: x: 4, y: 8, z: 8, core: 2. Of those that a mesh axis runs over, the one named last changes fastest.
Arguments:
- tokens: bfloat16 [512, 8192], P('col', 'row'), may hold values from -24 to 24
- scales: float32 [8192], P('row'), may hold values from 0.25 to 4
- gate_weight: bfloat16 [8192, 16384], P('row', 'col'), may hold values from -0.0625 to 0.0625
- up_weight: bfloat16 [8192, 16384], P('row', 'col'), may hold values from -0.0625 to 0.0625
- down_weight: bfloat16 [16384, 8192], P('col', 'row'), may hold values from -0.046875 to 0.046875
- gate_mask: int32 [64, 128], P('row', 'col'), may hold values 0 or 1
- up_mask: int32 [64, 128], P('row', 'col'), may hold values 0 or 1
- down_mask: int32 [128, 64], P('col', 'row'), may hold values 0 or 1
- cotangent: bfloat16 [512, 8192], P('col', 'row'), may hold values from -4 to 4
Outputs:
- output: bfloat16 [512, 8192], P('col', 'row')
- input_grad: bfloat16 [512, 8192], P('col', 'row')
- gate_grad: bfloat16 [8192, 16384], P('row', 'col')
- up_grad: bfloat16 [8192, 16384], P('row', 'col')
- down_grad: bfloat16 [16384, 8192], P('col', 'row')
Inputs may be any that keep to these rules, and one draw needn't show every extreme that they name: gate_mask is 1 where a 128 x 128 tile of gate_weight is kept and 0 where it is pruned. up_mask is 1 where a tile of up_weight is kept and 0 where it is pruned. down_mask is 1 where a tile of down_weight is kept and 0 where it is pruned.
All inputs are finite; a program needn't handle non-finite values. No bound on the sum of `gate_mask` or of `up_mask` or of `down_mask` on one device may be relied on, other than what follows from the above.
Results may differ from a plain program's by a relative error of at most 0.039.
Values may be sent and summed in bfloat16 or wider, within the bound.
No kernel may reach another device: no remote copies, remote signals or barrier semaphores. Data moves between devices by JAX's collectives and lax.ppermute only.
A program may use at most 64 MiB of HBM per device.

v0:
```python
import jax
import jax.numpy as jnp
from jax import lax
from jax.sharding import PartitionSpec as P

D = 8192
TILE = 128
clip_ratio = 1.5


def expand(mask):
    return jnp.repeat(jnp.repeat(mask, TILE, axis=0), TILE, axis=1).astype(jnp.float32)


def contract_last(left, right):
    return lax.dot_general(
        left, right, (((1,), (1,)), ((), ())), preferred_element_type=jnp.float32
    )


def contract_first(left, right):
    return lax.dot_general(
        left, right, (((0,), (0,)), ((), ())), preferred_element_type=jnp.float32
    )


def clip_tokens(smoothed, squares):
    limits = clip_ratio * jnp.sqrt(squares / D + 1e-06)[:, None]
    squashed = jnp.tanh(smoothed / limits)
    return (squashed, (limits * squashed).astype(jnp.bfloat16))


def swiglu_parts(gate_pre):
    sigmoid_gate = jax.nn.sigmoid(gate_pre)
    silu_gate = gate_pre * sigmoid_gate
    return (sigmoid_gate, silu_gate)


def swiglu_grads(hidden_grad, gate_pre, up_pre):
    sigmoid_gate, silu_gate = swiglu_parts(gate_pre)
    gate_dir = (
        hidden_grad * up_pre * sigmoid_gate * (1.0 + gate_pre * (1.0 - sigmoid_gate))
    ).astype(jnp.bfloat16)
    up_dir = (hidden_grad * silu_gate).astype(jnp.bfloat16)
    return jnp.concatenate([gate_dir, up_dir], axis=1)


def per_device(
    tokens, scales, gate_weight, up_weight, down_weight, gate_mask, up_mask, down_mask, cotangent
):
    hidden_width = gate_weight.shape[1]
    gate_keep = expand(gate_mask)
    up_keep = expand(up_mask)
    down_keep = expand(down_mask)
    gate_kept = (scales[:, None] * gate_weight.astype(jnp.float32) * gate_keep).astype(jnp.bfloat16)
    up_kept = (scales[:, None] * up_weight.astype(jnp.float32) * up_keep).astype(jnp.bfloat16)
    down_kept = down_weight * down_keep.astype(jnp.bfloat16)
    both_kept = jnp.concatenate([gate_kept, up_kept], axis=1)
    smoothed = tokens.astype(jnp.float32) / scales
    squares = lax.psum(jnp.sum(smoothed * smoothed, axis=1), "row")
    squashed, quantized = clip_tokens(smoothed, squares)
    quantized_all = lax.all_gather(quantized, "col", axis=0, tiled=True)
    picked = quantized_all
    gate_up = lax.psum(
        jnp.dot(picked, both_kept, preferred_element_type=jnp.float32).astype(jnp.bfloat16), "row"
    ).astype(jnp.float32)
    gate_pre = gate_up[:, :hidden_width]
    up_pre = gate_up[:, hidden_width:]
    sigmoid_gate, silu_gate = swiglu_parts(gate_pre)
    hidden_all = (silu_gate * up_pre).astype(jnp.bfloat16)
    picked = hidden_all
    output = lax.psum_scatter(
        jnp.dot(picked, down_kept, preferred_element_type=jnp.float32).astype(jnp.bfloat16),
        "col",
        scatter_dimension=0,
        tiled=True,
    )
    cotangent_all = lax.all_gather(cotangent, "col", axis=0, tiled=True)
    down_grad = (contract_first(hidden_all, cotangent_all) * down_keep).astype(jnp.bfloat16)
    picked = cotangent_all
    hidden_grad = lax.psum(contract_last(picked, down_kept).astype(jnp.bfloat16), "row").astype(
        jnp.float32
    )
    both_dirs_all = swiglu_grads(hidden_grad, gate_pre, up_pre)
    picked = both_dirs_all
    quant_grad = lax.psum_scatter(
        contract_last(picked, both_kept).astype(jnp.bfloat16),
        "col",
        scatter_dimension=0,
        tiled=True,
    ).astype(jnp.float32)
    input_grad = (quant_grad * (1.0 - squashed * squashed) / scales).astype(jnp.bfloat16)
    weight_product = contract_first(quantized_all, both_dirs_all)
    gate_grad = (scales[:, None] * weight_product[:, :hidden_width] * gate_keep).astype(
        jnp.bfloat16
    )
    up_grad = (scales[:, None] * weight_product[:, hidden_width:] * up_keep).astype(jnp.bfloat16)
    return (output, input_grad, gate_grad, up_grad, down_grad)


def solution(mesh):
    placed = (
        P("col", "row"),
        P("row"),
        P("row", "col"),
        P("row", "col"),
        P("col", "row"),
        P("row", "col"),
        P("row", "col"),
        P("col", "row"),
        P("col", "row"),
    )
    return jax.shard_map(
        per_device,
        mesh=mesh,
        in_specs=placed,
        out_specs=(
            P("col", "row"),
            P("col", "row"),
            P("row", "col"),
            P("row", "col"),
            P("col", "row"),
        ),
        check_vma=False,
    )
```

profile of v0, /device:TPU:16, one launch (start us, length us, event | category | flops | bytes accessed | tf_op | source)
XLA Modules:
  0.0 713.3 jit_solution(10551113524191224439)
XLA Ops:
  7.2 0.9 fusion.15
  8.1 32.0 %psum.21 = f32[16]{0:T(128)S(1)} all-reduce(f32[16]{0:T(128)S(1)} %fusion.15), channel_id=1, replica_groups=mesh['row'=16,'col'=32] {'row'}, use_global_device_ids=true, to_apply=%region_1.0 | all-reduce | flops 16 | bytes 128 | tf_op jit(solution)/shard_map/psum | solution.py:60
  40.1 0.7 convert_element_type.102
  40.8 0.7 convert_element_type.107
  41.5 0.7 convert_element_type.114
  42.2 0.8 multiply_convert_fusion.1
  43.0 50.1 %all_gather.6 = bf16[512,512]{1,0:T(8,128)(2,1)S(1)} all-gather(bf16[16,512]{1,0:T(8,128)(2,1)S(1)} %multiply_convert_fusion.1), channel_id=1, replica_groups=mesh['row'=16,'col'=32] {'col'}, dimensions={0}, use_global_device_ids=true | all-gather | bytes 540672 | tf_op jit(solution)/shard_map/all_gather | solution.py:62
  93.1 47.0 %all_gather.7 = bf16[512,512]{1,0:T(8,128)(2,1)S(1)} all-gather(bf16[16,512]{1,0:T(8,128)(2,1)} %param.17), channel_id=1, replica_groups=mesh['row'=16,'col'=32] {'col'}, dimensions={0}, use_global_device_ids=true | all-gather | bytes 540672 | tf_op jit(solution)/shard_map/all_gather | solution.py:78
  140.7 1.3 fusion.1
  142.0 0.6 broadcast_in_dim.26
  143.7 0.8 copy-done.9
  144.6 1.7 convolution_convert_fusion
  146.4 114.4 %all-reduce.3.cloned.1.call-done = (bf16[512,1024]{1,0:T(8,128)(2,1)}, bf16[512,512]{1,0:T(8,128)(2,1)}) async-done(((bf16[512,1024]{1,0:T(8,128)(2,1)}, bf16[512,512]{1,0:T(8,128)(2,1)}), (bf16[512,1024]{1,0:T(8,128)(2,1)}, bf16[512,512]{1,0:T(8,128)(2,1)})) %all-reduce.3.cloned.1.call-update) | async-done | bytes 1572880 | tf_op jit(solution)/shard_map/psum | solution.py:64
  260.8 1.5 convert_element_type.112
  262.4 1.4 fusion.4
  263.8 0.8 copy-done.3
  264.8 1.6 convolution_convert_fusion.3
  266.4 2.5 convolution_convert_fusion.2
  269.0 2.6 fusion
  271.5 0.7 fusion.11
  272.3 1.2 fusion.7
  273.5 210.9 %reduce-scatter.5.cloned.1.call-done = bf16[16,512]{1,0:T(8,128)(2,1)} async-done(((bf16[512,512]{1,0:T(8,128)(2,1)}), bf16[16,512]{1,0:T(8,128)(2,1)}) %reduce-scatter.5.cloned.1.call-update) | async-done | bytes 16400 | tf_op jit(solution)/shard_map/reduce_scatter | solution.py:86
  484.5 1.4 divide_convert_fusion
  485.9 220.9 %reduce-scatter.3.cloned.1.call-done = bf16[16,512]{1,0:T(8,128)(2,1)} async-done(((bf16[512,512]{1,0:T(8,128)(2,1)}), bf16[16,512]{1,0:T(8,128)(2,1)}) %reduce-scatter.3.cloned.1.call-update) | async-done | bytes 16400 | tf_op jit(solution)/shard_map/reduce_scatter | solution.py:72
  (45 shorter events, 2.2 us)
Async XLA Ops:
  7.2 133.6 %copy-start.16 = (bf16[512,512]{1,0:T(8,128)(2,1)S(1)}, bf16[512,512]{1,0:T(8,128)(2,1)}, u32[]{:S(2)}) copy-start(bf16[512,512]{1,0:T(8,128)(2,1)} %param.13) | copy-start | bytes 1572868
  7.2 253.6 %all-reduce.3.cloned.1.call-start = ((), (), s32[]{:S(2)}) async-start(), calls=%async_computation.4 | async-start | bytes 3145728 | tf_op jit(solution)/shard_map/psum | solution.py:64
  93.1 50.6 %copy-start = (bf16[512,512]{1,0:T(8,128)(2,1)}, bf16[512,512]{1,0:T(8,128)(2,1)S(1)}, u32[]{:S(2)}) copy-start(bf16[512,512]{1,0:T(8,128)(2,1)S(1)} %all_gather.6) | copy-start | bytes 1572868
  140.1 1.9 copy-start.2
  142.0 1.3 copy-start.7
  142.0 1.3 copy-start.8
  142.0 1.3 copy-start.15
  143.6 0.8 copy-start.9
  143.6 1.0 copy-start.11
  146.3 338.1 %reduce-scatter.5.cloned.1.call-start = ((), (), s32[]{:S(2)}) async-start(), calls=%async_computation.3 | async-start | bytes 540672 | tf_op jit(solution)/shard_map/reduce_scatter | solution.py:86
  260.8 1.5 copy-start.13
  262.3 2.4 copy-start.10
  262.4 2.4 copy-start.12
  263.8 0.8 copy-start.3
  263.8 1.0 copy-start.5
  266.4 440.4 %reduce-scatter.3.cloned.1.call-start = ((), (), s32[]{:S(2)}) async-start(), calls=%async_computation.2 | async-start | bytes 540672 | tf_op jit(solution)/shard_map/reduce_scatter | solution.py:72
  268.9 2.6 copy-start.1
  268.9 2.6 copy-start.4
  268.9 2.6 copy-start.6
  272.3 212.2 %copy-start.14 = (bf16[16,512]{1,0:T(8,128)(2,1)S(1)}, bf16[16,512]{1,0:T(8,128)(2,1)}, u32[]{:S(2)}) copy-start(bf16[16,512]{1,0:T(8,128)(2,1)} %param.9) | copy-start | bytes 49156
Sparse Core Ops, SparseCore 0:
  146.4 114.3 all-reduce.2
  266.5 217.9 reduce-scatter.4
  489.4 217.3 reduce-scatter.2
where the time goes:
time: 714 us; the launch traced here: 713 us
  waiting for transfers between devices  546 us (76%)
  blocking collectives  129 us (18%)
  between operations  13.9 us (2%)
  matrix products  10.3 us (1%)
  other arithmetic  9.67 us (1%)
    reduce_scatter x1, waiting for transfers between devices, per_device(): lax.psum_scatter(jnp.dot(picked, down_kept, preferred_element_type=jnp.fl...  221 us
    reduce_scatter x1, waiting for transfers between devices, per_device(): lax.psum_scatter(contract_last(picked, both_kept).astype(jnp.bfloat16), '...  211 us
    psum x1, waiting for transfers between devices, per_device(): lax.psum(jnp.dot(picked, both_kept, preferred_element_type=jnp.float32).a...  114 us
    all_gather x1, blocking collectives, per_device(): quantized_all = lax.all_gather(quantized, 'col', axis=0, tiled=True)  50.1 us
    all_gather x1, blocking collectives, per_device(): cotangent_all = lax.all_gather(cotangent, 'col', axis=0, tiled=True)  47 us
    psum x1, blocking collectives, per_device(): squares = lax.psum(jnp.sum(smoothed * smoothed, axis=1), 'row')  32 us
  transfers between devices with their start and end apart: 3, of which 3 were waited for; matrix products, arithmetic and copies ran while one was open for 1% of the time, Pallas kernels for 0%

commit v1 on v0

--- a/solution.py
+++ b/solution.py
@@ -61,9 +61,14 @@
     squashed, quantized = clip_tokens(smoothed, squares)
     quantized_all = lax.all_gather(quantized, "col", axis=0, tiled=True)
     picked = quantized_all
-    gate_up = lax.psum(
-        jnp.dot(picked, both_kept, preferred_element_type=jnp.float32).astype(jnp.bfloat16), "row"
-    ).astype(jnp.float32)
+    gate_up = (
+        jax.lax.all_gather(
+            jnp.dot(picked, both_kept, preferred_element_type=jnp.float32).astype(jnp.bfloat16),
+            "row",
+        )
+        .sum(axis=0)
+        .astype(jnp.float32)
+    )
     gate_pre = gate_up[:, :hidden_width]
     up_pre = gate_up[:, hidden_width:]
     sigmoid_gate, silu_gate = swiglu_parts(gate_pre)

time: 714 us -> 759 us (1.063)
  waiting for transfers between devices: 546 us -> 577 us
  other arithmetic: 9.67 us -> 21.5 us
    all_gather x0 -> x1, waiting for transfers between devices: none -> 42.1 us  [per_device(): jax.lax.all_gather(jnp.dot(picked, both_kept, preferred_element_type=jnp....]
    psum x1, waiting for transfers between devices: 114 us -> 103 us  [per_device(): lax.psum(contract_last(picked, down_kept).astype(jnp.bfloat16), 'row')]
    reduce_sum x0 -> x1, other arithmetic: none -> 9.33 us  [per_device(): gate_up = jax.lax.all_gather(jnp.dot(picked, both_kept, preferred_element...]
  transfers between devices with their start and end apart: 3 -> 4, of which waited for: 3 -> 4; matrix products, arithmetic and copies ran while one was open for 1% -> 3% of each run, Pallas kernels for 0% -> 0%
where the time goes in v1:
time: 759 us
  waiting for transfers between devices  577 us (76%)
  blocking collectives  129 us (17%)
  other arithmetic  21.5 us (3%)
  between operations  14 us (2%)
  matrix products  10.5 us (1%)
    reduce_scatter x1, waiting for transfers between devices, per_device(): lax.psum_scatter(jnp.dot(picked, down_kept, preferred_element_type=jnp.fl...  221 us
    reduce_scatter x1, waiting for transfers between devices, per_device(): lax.psum_scatter(contract_last(picked, both_kept).astype(jnp.bfloat16), '...  211 us
    psum x1, waiting for transfers between devices, per_device(): lax.psum(contract_last(picked, down_kept).astype(jnp.bfloat16), 'row')  103 us
    all_gather x1, blocking collectives, per_device(): quantized_all = lax.all_gather(quantized, 'col', axis=0, tiled=True)  50.1 us
    all_gather x1, blocking collectives, per_device(): cotangent_all = lax.all_gather(cotangent, 'col', axis=0, tiled=True)  47.2 us
    all_gather x1, waiting for transfers between devices, per_device(): jax.lax.all_gather(jnp.dot(picked, both_kept, preferred_element_type=jnp....  42.1 us
    psum x1, blocking collectives, per_device(): squares = lax.psum(jnp.sum(smoothed * smoothed, axis=1), 'row')  32 us
  transfers between devices with their start and end apart: 4, of which 4 were waited for; matrix products, arithmetic and copies ran while one was open for 3% of the time, Pallas kernels for 0%

profile of v1, /device:TPU:16, one launch (start us, length us, event | category | flops | bytes accessed | tf_op | source)
XLA Modules:
  0.0 758.5 jit_solution(18401673958982274752)
XLA Ops:
  7.2 0.8 convert_element_type.104
  8.7 0.8 fusion.15
  9.5 32.0 %psum.14 = f32[16]{0:T(128)S(1)} all-reduce(f32[16]{0:T(128)S(1)} %fusion.15), channel_id=1, replica_groups=mesh['row'=16,'col'=32] {'row'}, use_global_device_ids=true, to_apply=%region_1.0 | all-reduce | flops 16 | bytes 128 | tf_op jit(solution)/shard_map/psum | solution.py:60
  41.6 0.8 multiply_convert_fusion.1
  42.4 50.1 %all_gather.12 = bf16[512,512]{1,0:T(8,128)(2,1)S(1)} all-gather(bf16[16,512]{1,0:T(8,128)(2,1)S(1)} %multiply_convert_fusion.1), channel_id=1, replica_groups=mesh['row'=16,'col'=32] {'col'}, dimensions={0}, use_global_device_ids=true | all-gather | bytes 540672 | tf_op jit(solution)/shard_map/all_gather | solution.py:62
  95.0 1.7 convolution_convert_fusion
  96.8 47.2 %all_gather.15 = bf16[512,512]{1,0:T(8,128)(2,1)S(1)} all-gather(bf16[16,512]{1,0:T(8,128)(2,1)S(1)} %copy-done.16), channel_id=1, replica_groups=mesh['row'=16,'col'=32] {'col'}, dimensions={0}, use_global_device_ids=true | all-gather | bytes 540672 | tf_op jit(solution)/shard_map/all_gather | solution.py:83
  144.8 0.8 copy-done
  145.6 1.3 fusion.1
  146.9 42.1 %all-gather.3.cloned.1.call-done = bf16[8192,1024]{1,0:T(8,128)(2,1)} async-done(((bf16[512,1024]{1,0:T(8,128)(2,1)}), bf16[8192,1024]{1,0:T(8,128)(2,1)}) %all-gather.3.cloned.1.call-update) | async-done | bytes 16777232 | tf_op jit(solution)/shard_map/all_gather | solution.py:65
  189.0 9.3 %reduce_sum.22 = bf16[512,1024]{1,0:T(8,128)(2,1)S(1)} reduce(bf16[16,512,1024]{2,1,0:T(8,128)(2,1)} %bitcast.36, bf16[]{:T(256)} %constant.12.clone.1), dimensions={0}, to_apply=%region_2.0 | reduce | flops 7864320 | bytes 17825794 | tf_op jit(solution)/shard_map/reduce_sum | solution.py:69
  198.4 1.3 copy.14
  199.7 2.8 convert_element_type.114
  202.5 103.2 %all-reduce.2.cloned.1.call-done = bf16[512,512]{0,1:T(8,128)(2,1)} async-done(((bf16[512,512]{0,1:T(8,128)(2,1)}), bf16[512,512]{0,1:T(8,128)(2,1)}) %all-reduce.2.cloned.1.call-update) | async-done | bytes 524304 | tf_op jit(solution)/shard_map/psum | solution.py:86
  305.8 3.2 fusion.4
  309.0 0.8 copy-done.6
  310.0 1.6 convolution_convert_fusion.3
  311.7 2.5 convolution_convert_fusion.2
  314.2 2.2 fusion.11
  316.4 1.2 fusion
  317.7 1.2 fusion.7
  318.9 211.0 %reduce-scatter.5.cloned.1.call-done = bf16[16,512]{1,0:T(8,128)(2,1)} async-done(((bf16[512,512]{1,0:T(8,128)(2,1)}), bf16[16,512]{1,0:T(8,128)(2,1)}) %reduce-scatter.5.cloned.1.call-update) | async-done | bytes 16400 | tf_op jit(solution)/shard_map/reduce_scatter | solution.py:91
  529.9 1.4 divide_convert_fusion
  531.3 220.7 %reduce-scatter.3.cloned.1.call-done = bf16[16,512]{1,0:T(8,128)(2,1)} async-done(((bf16[512,512]{1,0:T(8,128)(2,1)}), bf16[16,512]{1,0:T(8,128)(2,1)}) %reduce-scatter.3.cloned.1.call-update) | async-done | bytes 16400 | tf_op jit(solution)/shard_map/reduce_scatter | solution.py:77
  (54 shorter events, 4.4 us)
Async XLA Ops:
  7.2 86.5 %copy-start.15 = (f32[512]{0:T(512)S(1)}, f32[512]{0:T(512)}, u32[]{:S(2)}) copy-start(f32[512]{0:T(512)} %param.10) | copy-start | bytes 6148
  7.2 86.5 %copy-start.8 = (bf16[512,512]{1,0:T(8,128)(2,1)S(1)}, bf16[512,512]{1,0:T(8,128)(2,1)}, u32[]{:S(2)}) copy-start(bf16[512,512]{1,0:T(8,128)(2,1)} %param.11) | copy-start | bytes 1572868
  7.2 86.5 %copy-start.9 = (bf16[512,512]{1,0:T(8,128)(2,1)S(1)}, bf16[512,512]{1,0:T(8,128)(2,1)}, u32[]{:S(2)}) copy-start(bf16[512,512]{1,0:T(8,128)(2,1)} %param.12) | copy-start | bytes 1572868
  7.2 181.8 %all-gather.3.cloned.1.call-start = ((), (), s32[]{:S(2)}) async-start(), calls=%async_computation.5 | async-start | bytes 17825792 | tf_op jit(solution)/shard_map/all_gather | solution.py:65
  92.4 1.6 copy-start.2
  94.0 0.8 copy-start.10
  94.0 1.0 copy-start.12
  95.0 1.8 copy-start.17
  95.0 1.8 copy-start.16
  96.7 48.9 %copy-start.18 = (bf16[512,512]{1,0:T(8,128)(2,1)S(1)}, bf16[512,512]{1,0:T(8,128)(2,1)}, u32[]{:S(2)}) copy-start(bf16[512,512]{1,0:T(8,128)(2,1)} %param.13) | copy-start | bytes 1572868
  96.7 209.0 %all-reduce.2.cloned.1.call-start = ((), (), s32[]{:S(2)}) async-start(), calls=%async_computation.3 | async-start | bytes 1048576 | tf_op jit(solution)/shard_map/psum | solution.py:86
  144.0 0.8 copy-start.3
  144.6 1.0 copy-start
  146.9 383.0 %reduce-scatter.5.cloned.1.call-start = ((), (), s32[]{:S(2)}) async-start(), calls=%async_computation.4 | async-start | bytes 540672 | tf_op jit(solution)/shard_map/reduce_scatter | solution.py:91
  305.8 4.2 copy-start.11
  305.8 4.2 copy-start.13
  309.0 0.8 copy-start.6
  309.0 1.0 copy-start.7
  310.0 1.7 copy-start.1
  311.6 440.4 %reduce-scatter.3.cloned.1.call-start = ((), (), s32[]{:S(2)}) async-start(), calls=%async_computation.2 | async-start | bytes 540672 | tf_op jit(solution)/shard_map/reduce_scatter | solution.py:77
  314.2 2.2 copy-start.4
  314.2 2.2 copy-start.5
  317.7 212.2 %copy-start.14 = (bf16[16,512]{1,0:T(8,128)(2,1)S(1)}, bf16[16,512]{1,0:T(8,128)(2,1)}, u32[]{:S(2)}) copy-start(bf16[16,512]{1,0:T(8,128)(2,1)} %param.9) | copy-start | bytes 49156
Sparse Core Ops, SparseCore 0:
  96.8 92.1 all-gather.2
  191.9 113.8 all-reduce.1
  311.7 218.1 reduce-scatter.4
  534.7 217.2 reduce-scatter.2
